TPU v7x, 256 devices: a whole 4x4x8 slice. The times are simulated.
256 devices in a mesh: dp: 16 (over x, z_hi, core), seq: 16 (over y, z_lo).
Axes of the slice: x: 4, y: 4, z: 8 (z_hi: 2, z_lo: 4; z = z_hi * 4 + z_lo), core: 2. Of those that a mesh axis runs over, the one named last changes fastest.
Arguments:
- tokens: bfloat16 [16, 2048, 1024], P('dp', 'seq'), may hold values from -6 to 6
- in_gain: float32 [1024], replicated, may hold values from 0.1 to 1.9
- w_proj: bfloat16 [1024, 4096], replicated, may hold values from -0.1875 to 0.1875
- out_gain: float32 [1024], replicated, may hold values from 0.1 to 1.9
- w_out: bfloat16 [1024, 1024], replicated, may hold values from -0.1875 to 0.1875
- rab_slope: float32 [8], replicated, may hold values from -1 to 0.2
- hist_blocks: int32 [16, 3], P('dp'), may hold values from 1 to 10, 16 in all within a row
- hist_tail: int32 [16, 3], P('dp'), may hold values from 1 to 128
- node_table: bfloat16 [4096, 1024], P('dp'), may hold values from -0.1875 to 0.1875
- subtree_map: int32 [64], replicated, may hold values from 0 to 63, each once
- beam_nodes: int32 [48, 1024], P('dp', 'seq'), may hold values from 0 to 4095
Outputs:
- layer_out: bfloat16 [16, 2048, 1024], P('dp', 'seq')
- beam_scores: float32 [48, 1024], P('dp', 'seq')
Inputs may be any that keep to these rules, and one draw needn't show every extreme that they name: `hist_blocks`: each row sums to 16; its largest entry is exactly 10. `subtree_map`: a permutation of 0 to 63.
All inputs are finite; a program needn't handle non-finite values.
Results may differ from a plain program's by a relative error of at most 0.0059.
Values may be sent and summed in bfloat16 or wider, within the bound.
No kernel may reach another device: no remote copies, remote signals or barrier semaphores. Data moves between devices by JAX's collectives and lax.ppermute only.
A program may use at most 128 MiB of HBM per device.

v0:
```python
import jax
import jax.numpy as jnp
from jax import lax
from jax.sharding import PartitionSpec as P

BLK = 128
SUBT = 64
USERS = 3


def layer_norm(rows):
    centred = rows - jnp.mean(rows, axis=-1, keepdims=True)
    spread = jnp.mean(centred * centred, axis=-1, keepdims=True)
    return centred * lax.rsqrt(spread + 1e-05)


def user_table(blocks, tail_len):
    starts = jnp.cumsum(blocks) - blocks
    lengths = (blocks - 1) * BLK + tail_len
    return (starts, lengths)


def segments(blocks, tail_len, positions):
    starts, lengths = user_table(blocks, tail_len)
    block_of = jnp.floor_divide(positions, BLK)
    owning = jnp.sum((block_of[:, None] >= starts[None, :]).astype(jnp.int32), axis=1) - 1
    onehot = (owning[:, None] == jnp.arange(USERS, dtype=jnp.int32)[None, :]).astype(jnp.int32)
    first_pos = jnp.sum(onehot * starts[None, :], axis=1) * BLK
    user_len = jnp.sum(onehot * lengths[None, :], axis=1)
    is_live = (owning >= 0) & (positions - first_pos < user_len)
    return jnp.where(is_live, owning, -1)


def attend(queries, query_pos, query_seg, key_rows, value_rows, key_pos, key_seg, rab_slope):
    scores = jnp.einsum("qhd,khd->hqk", queries, key_rows, preferred_element_type=jnp.float32)
    scores = scores * queries.shape[-1] ** (-0.5)
    gap = query_pos[:, None] - key_pos[None, :]
    allowed = (query_seg[:, None] == key_seg[None, :]) & (query_seg[:, None] >= 0) & (gap >= 0)
    bias = rab_slope[:, None, None] * jnp.log1p(jnp.maximum(gap, 0).astype(jnp.float32))[None]
    weights = jnp.where(allowed[None], jax.nn.silu(scores + bias), 0.0).astype(jnp.bfloat16)
    return jnp.einsum("hqk,khd->qhd", weights, value_rows, preferred_element_type=jnp.float32)


def body(
    tokens,
    in_gain,
    w_proj,
    out_gain,
    w_out,
    rab_slope,
    hist_blocks,
    hist_tail,
    node_table,
    subtree_map,
    beam_nodes,
):
    x_rows = tokens[0]
    tok_dev, width = x_rows.shape
    heads = rab_slope.shape[0]
    head_dim = width // heads
    seq_index = lax.axis_index("seq")
    blocks = hist_blocks[0]
    tail_len = hist_tail[0]
    normed = (layer_norm(x_rows.astype(jnp.float32)) * in_gain).astype(jnp.bfloat16)
    proj = jax.nn.silu(jnp.dot(normed, w_proj, preferred_element_type=jnp.float32)).astype(
        jnp.bfloat16
    )
    gate_rows = proj[:, :width]
    queries = proj[:, width : 2 * width].reshape(tok_dev, heads, head_dim)
    key_value = proj[:, 2 * width :]
    query_pos = seq_index * tok_dev + jnp.arange(tok_dev, dtype=jnp.int32)
    query_seg = segments(blocks, tail_len, query_pos)
    empty = jnp.zeros((tok_dev, heads, head_dim), jnp.float32)
    piece = lax.all_gather(key_value, "seq", axis=0, tiled=True)
    count = piece.shape[0]
    key_pos = jnp.arange(count, dtype=jnp.int32)
    key_seg = segments(blocks, tail_len, key_pos)
    touching = (query_seg[:, None] == key_seg[None, :]) & (query_seg[:, None] >= 0)
    touching = touching & (query_pos[:, None] >= key_pos[None, :])

    def compute(acc):
        key_rows = piece[:, :width].reshape(count, heads, head_dim)
        value_rows = piece[:, width:].reshape(count, heads, head_dim)
        return attend(
            queries, query_pos, query_seg, key_rows, value_rows, key_pos, key_seg, rab_slope
        )

    mixed = lax.cond(jnp.any(touching), compute, lambda acc: acc, empty)
    mixed = mixed.reshape(tok_dev, width)
    gated = (layer_norm(mixed) * out_gain * gate_rows.astype(jnp.float32)).astype(jnp.bfloat16)
    layer_rows = (
        x_rows.astype(jnp.float32) + jnp.dot(gated, w_out, preferred_element_type=jnp.float32)
    ).astype(jnp.bfloat16)
    starts, lengths = user_table(blocks, tail_len)
    local_last = starts * BLK + lengths - 1 - seq_index * tok_dev
    picker = (jnp.arange(tok_dev, dtype=jnp.int32)[None, :] == local_last[:, None]).astype(
        jnp.bfloat16
    )
    state_part = jnp.dot(picker, layer_rows, preferred_element_type=jnp.float32)
    dp_index = lax.axis_index("dp")
    state_rows = lax.psum(state_part, "seq").astype(jnp.bfloat16)
    all_states, all_ids = (
        lax.all_gather(state_rows, "dp", axis=0, tiled=True),
        lax.all_gather(beam_nodes, "dp", axis=0, tiled=True),
    )
    nodes_here = node_table.shape[0]
    stored = jnp.take(subtree_map, all_ids // SUBT) * SUBT + all_ids % SUBT
    local_rows = stored - dp_index * nodes_here
    owned = (local_rows >= 0) & (local_rows < nodes_here)
    local_scores = lax.dot_general(
        all_states, node_table, (((1,), (1,)), ((), ())), preferred_element_type=jnp.float32
    )
    picked = jnp.take_along_axis(local_scores, jnp.clip(local_rows, 0, nodes_here - 1), axis=1)
    picked = jnp.where(owned, picked, 0.0)
    beam_scores = lax.psum_scatter(picked, "dp", scatter_dimension=0, tiled=True)
    return (layer_rows[None], beam_scores)


def solution(mesh):
    placed = (
        P("dp", "seq", None),
        P(),
        P(),
        P(),
        P(),
        P(),
        P("dp", None),
        P("dp", None),
        P("dp", None),
        P(),
        P("dp", "seq"),
    )
    return jax.shard_map(
        body,
        mesh=mesh,
        in_specs=placed,
        out_specs=(P("dp", "seq", None), P("dp", "seq")),
        check_vma=False,
    )
```

profile of v0, /device:TPU:0, one launch (start us, length us, event | category | flops | bytes accessed | tf_op | source)
XLA Modules:
  0.0 461.4 jit_solution(8129553913338735641)
XLA Ops:
  7.2 1.2 convert_reduce_fusion
  8.4 1.2 fusion.16
  9.7 5.0 %multiply_convert_fusion = bf16[128,4096]{1,0:T(8,128)(2,1)S(1)} fusion(bf16[1024,4096]{1,0:T(8,128)(2,1)} %param.15, bf16[1,128,1024]{2,1,0:T(8,128)(2,1)} %param.13, f32[1024]{0:T(1024)} %param.14, f32[128]{0:T(128)S(1)} %add_rsqrt_fusion.1, f32[128]{0:T(128)S(1)} %broadcast_multiply_fusion.1), kind=kOutput, calls=%fused_computation.18 | convolution fusion | flops 1077018624 | bytes 9704448 | tf_op jit(solution)/shard_map/dot_general | solution.py:65
  14.6 1.1 copy-done.2
  15.7 0.9 slice.25
  16.6 0.2 reduce-window.4
  16.9 0.1 convert_reduce_fusion.1
  17.1 0.1 select_reduce_fusion.1
  17.3 1.0 fusion.12
  19.0 32.1 %all-gather = s32[16,3,64]{2,1,0:T(4,128)S(1)} all-gather(s32[1,3,64]{2,1,0:T(4,128)S(1)} %bitcast.96), channel_id=1, replica_groups=mesh['dp'=16,'seq'=16] {'dp'}, dimensions={0}, use_global_device_ids=true | all-gather | bytes 13056 | tf_op jit(solution)/shard_map/all_gather | solution.py:104
  51.2 18.7 %gather_fusion = s32[3072]{0:T(1024)S(1)} fusion(s32[64]{0:T(128)S(1)} %copy-done.1, s32[3072]{0:T(1024)S(1)} %broadcast_clamp_fusion), kind=kCustom, calls=%fused_computation | custom fusion | bytes 36864 | tf_op jit(solution)/shard_map/jit(_take)/gather | solution.py:107
  70.1 0.6 dynamic-slice
  71.3 132.7 %all-gather.4.cloned.1.call-done = bf16[2048,2048]{1,0:T(8,128)(2,1)} async-done(((bf16[128,2048]{1,0:T(8,128)(2,1)}), bf16[2048,2048]{1,0:T(8,128)(2,1)}) %all-gather.4.cloned.1.call-update) | async-done | bytes 8388624 | tf_op jit(solution)/shard_map/all_gather | solution.py:74
  204.1 29.9 %conditional.1 = (f32[128,8,128]{2,0,1:T(8,128)S(1)}) conditional(s32[]{:T(128)} %convert_element_type.51, () %tuple.14, (s32[128]{0:T(128)S(1)}, s32[128]{0:T(128)S(1)}, s32[128]{0:T(128)S(1)}, s32[128]{0:T(128)S(1)}, s32[128]{0:T(128)S(1)}, /*index=5*/s32[2048]{0:T(1024)S(1)}, s32[2048]{0:T(1024)S(1)}, s32[2048]{0:T(1024)S(1)}, ...), branch_computations={%region_10.11_spmd, %region_11.12_spmd} | conditional | flops 1094726528 | bytes 52245316 | solution.py:88
  204.1 12.4 %copy.31 = bf16[2048,2048]{0,1:T(8,128)(2,1)} copy(bf16[2048,2048]{1,0:T(8,128)(2,1)} %get-tuple-element.114) | data formatting | bytes 16777216 | tf_op jit(solution)/shard_map
  216.5 6.1 %fusion.53 = (bf16[2048,1024]{0,1:T(8,128)(2,1)}, bf16[2048,1024]{0,1:T(8,128)(2,1)}) fusion(bf16[2048,2048]{0,1:T(8,128)(2,1)} %copy.31), kind=kLoop, calls=%fused_computation.108 | loop fusion | bytes 16777216 | tf_op jit(solution)/shard_map/cond/branch_1_fun/slice | solution.py:82
  222.6 1.4 copy.30
  224.0 1.0 slice.22
  225.0 1.6 fusion.3
  226.6 0.4 fusion.4
  227.0 7.0 %fusion.1 = f32[128,8,128]{2,0,1:T(8,128)S(1)} fusion(bf16[2048,8,128]{0,2,1:T(8,128)(2,1)} %bitcast.92, bf16[128,8,128]{0,2,1:T(8,128)(2,1)S(1)} %bitcast.94, bf16[2048,8,128]{0,2,1:T(8,128)(2,1)} %bitcast.91, f32[128,2048]{1,0:T(8,128)} %fusion.3, f32[8]{0:T(128)S(1)} %get-tuple-element.73, pred[128,2048]{1,0:T(8,128)(4,1)S(1)} %fusion.4), kind=kOutput, calls=%fused_computation.6 | convolution fusion | flops 1092616192 | bytes 10485792 | tf_op jit(solution)/shard_map/cond/branch_1_fun/hqk,khd->qhd/dot_general | solution.py:41
  234.0 0.1 reduce_sum.98
  234.1 0.2 multiply_reduce_fusion
  234.4 1.5 fusion.10
  235.9 0.7 copy-done.6
  236.6 0.2 fusion.44
  236.8 75.5 %psum.7 = bf16[3,1024]{1,0:T(4,128)(2,1)S(1)} all-reduce(f32[3,1024]{1,0:T(4,128)S(1)} %fusion.44), channel_id=1, replica_groups=mesh['dp'=16,'seq'=16] {'seq'}, use_global_device_ids=true, to_apply=%region_14.15 | all-reduce | flops 3072 | bytes 18432 | tf_op jit(solution)/shard_map/psum | solution.py:101
  312.3 32.2 %all-gather.1 = bf16[16,3,1024]{2,1,0:T(4,128)(2,1)S(1)} all-gather(bf16[1,3,1024]{2,1,0:T(4,128)(2,1)S(1)} %bitcast.95), channel_id=1, replica_groups=mesh['dp'=16,'seq'=16] {'dp'}, dimensions={0}, use_global_device_ids=true | all-gather | bytes 104448 | tf_op jit(solution)/shard_map/all_gather | solution.py:103
  344.5 0.3 fusion.54
  344.8 24.7 %gather_fusion.1 = f32[3072]{0:T(1024)S(1)} fusion(f32[48,256]{1,0:T(8,128)S(1)} %fusion.54, s32[3072]{0:T(1024)S(1)} %reshape.285), kind=kCustom, calls=%fused_computation.1 | custom fusion | bytes 49152 | tf_op jit(solution)/shard_map/jit(take_along_axis)/gather | solution.py:113
  369.6 84.4 %all-reduce = f32[48,64]{1,0:T(8,128)S(1)} all-reduce(f32[48,64]{1,0:T(8,128)S(1)} %select_select_fusion), channel_id=2, replica_groups=mesh['dp'=16,'seq'=16] {'dp'}, use_global_device_ids=true, to_apply=%region_15.16.clone | all-reduce | flops 3072 | bytes 24576
  454.0 0.6 constant_dynamic-slice_fusion
  (55 shorter events, 0.9 us)
Async XLA Ops:
  7.2 227.2 %copy-start = (bf16[1024,1024]{1,0:T(8,128)(2,1)S(1)}, bf16[1024,1024]{1,0:T(8,128)(2,1)}, u32[]{:S(2)}) copy-start(bf16[1024,1024]{1,0:T(8,128)(2,1)} %param.17) | copy-start | bytes 6291460
  7.2 196.9 %all-gather.4.cloned.1.call-start = ((), (), s32[]{:S(2)}) async-start(), calls=%async_computation | async-start | bytes 8912896 | tf_op jit(solution)/shard_map/all_gather | solution.py:74
  9.6 7.0 %copy-start.10 = (s32[1,3]{1,0:T(1,128)S(1)}, s32[1,3]{1,0:T(1,128)}, u32[]{:S(2)}) copy-start(s32[1,3]{1,0:T(1,128)} %param.19) | copy-start | bytes 40
  9.6 7.2 %copy-start.9 = (s32[1,3]{1,0:T(1,128)S(1)}, s32[1,3]{1,0:T(1,128)}, u32[]{:S(2)}) copy-start(s32[1,3]{1,0:T(1,128)} %param.20) | copy-start | bytes 40
  9.6 9.3 %copy-start.8 = (s32[3,64]{1,0:T(4,128)S(1)}, s32[3,64]{1,0:T(4,128)}, u32[]{:S(2)}) copy-start(s32[3,64]{1,0:T(4,128)} %param.23) | copy-start | bytes 2308
  14.6 1.1 copy-start.2
  15.7 35.5 %copy-start.1 = (s32[64]{0:T(128)S(1)}, s32[64]{0:T(128)}, u32[]{:S(2)}) copy-start(s32[64]{0:T(128)} %param.22) | copy-start | bytes 772
  51.2 18.9 %copy-start.12 = (u32[256]{0:T(256)S(1)}, u32[256]{0:T(256)}, u32[]{:S(2)}) copy-start(u32[256]{0:T(256)} %constant.165) | copy-start | bytes 3076
  51.2 152.9 %copy-start.11 = (f32[8]{0:T(128)S(1)}, f32[8]{0:T(128)}, u32[]{:S(2)}) copy-start(f32[8]{0:T(128)} %param.18) | copy-start | bytes 100
  204.1 30.3 %copy-start.4 = (bf16[1,128,1024]{2,1,0:T(8,128)(2,1)S(1)}, bf16[1,128,1024]{2,1,0:T(8,128)(2,1)}, u32[]{:S(2)}) copy-start(bf16[1,128,1024]{2,1,0:T(8,128)(2,1)} %param.13) | copy-start | bytes 786436
  204.1 30.3 %copy-start.7 = (f32[1024]{0:T(1024)S(1)}, f32[1024]{0:T(1024)}, u32[]{:S(2)}) copy-start(f32[1024]{0:T(1024)} %param.16) | copy-start | bytes 12292
  216.5 6.1 %copy-start.3 = (bf16[128,4096]{1,0:T(8,128)(2,1)S(1)}, bf16[128,4096]{1,0:T(8,128)(2,1)}, u32[]{:S(2)}) copy-start(bf16[128,4096]{1,0:T(8,128)(2,1)} %get-tuple-element.113) | copy-start | bytes 3145732 | tf_op jit(solution)/shard_map/cond
  234.0 110.5 %copy-start.5 = (bf16[256,1024]{1,0:T(8,128)(2,1)S(1)}, bf16[256,1024]{1,0:T(8,128)(2,1)}, u32[]{:S(2)}) copy-start(bf16[256,1024]{1,0:T(8,128)(2,1)} %param.21) | copy-start | bytes 1572868
  235.9 0.7 copy-start.6
Sparse Core Ops, SparseCore 0:
  16.7 187.3 all-gather.3
where the time goes:
time: 462 us; the launch traced here: 461 us
  blocking collectives  224 us (48%)
  waiting for transfers between devices  133 us (29%)
  local copies, waits for them, and re-layouts  68.5 us (15%)
  between operations  15.6 us (3%)
  matrix products  13.9 us (3%)
  other arithmetic  6.46 us (1%)
    all_gather x1, waiting for transfers between devices, body(): piece = lax.all_gather(key_value, 'seq', axis=0, tiled=True)  133 us
    unnamed x1, blocking collectives  84.4 us
    psum x1, blocking collectives, body(): state_rows = lax.psum(state_part, 'seq').astype(jnp.bfloat16)  75.5 us
    all_gather x1, blocking collectives, body(): lax.all_gather(state_rows, 'dp', axis=0, tiled=True)  32.2 us
    all_gather x1, blocking collectives, body(): lax.all_gather(beam_nodes, 'dp', axis=0, tiled=True)  32.1 us
    gather x3, local copies, waits for them, and re-layouts, body(): jnp.take_along_axis(local_scores, jnp.clip(local_rows, 0, nodes_here - 1)...  24.9 us
    gather x2, local copies, waits for them, and re-layouts, body(): stored = jnp.take(subtree_map, all_ids // SUBT) * SUBT + all_ids % SUBT  18.7 us
    another operation x4, local copies, waits for them, and re-layouts  13.8 us
  transfers between devices with their start and end apart: 1, of which 1 were waited for; matrix products, arithmetic and copies ran while one was open for 5% of the time, Pallas kernels for 0%

commit v1 on v0

--- a/solution.py
+++ b/solution.py
@@ -98,7 +98,7 @@
     )
     state_part = jnp.dot(picker, layer_rows, preferred_element_type=jnp.float32)
     dp_index = lax.axis_index("dp")
-    state_rows = lax.psum(state_part, "seq").astype(jnp.bfloat16)
+    state_rows = jnp.sum(lax.all_gather(state_part, "seq"), axis=0).astype(jnp.bfloat16)
     all_states, all_ids = (
         lax.all_gather(state_rows, "dp", axis=0, tiled=True),
         lax.all_gather(beam_nodes, "dp", axis=0, tiled=True),

time: 462 us -> 426 us (0.922)
  blocking collectives: 224 us -> 189 us
    psum x1 -> x0, blocking collectives: 75.5 us -> none  [body(): state_rows = lax.psum(state_part, 'seq').astype(jnp.bfloat16)]
    all_gather x0 -> x1, blocking collectives: none -> 39.9 us  [body(): lax.all_gather(state_part, 'seq')]
where the time goes in v1:
time: 426 us
  blocking collectives  189 us (44%)
  waiting for transfers between devices  133 us (31%)
  local copies, waits for them, and re-layouts  68.5 us (16%)
  between operations  15.6 us (4%)
  matrix products  13.9 us (3%)
  other arithmetic  6.52 us (2%)
    all_gather x1, waiting for transfers between devices, body(): piece = lax.all_gather(key_value, 'seq', axis=0, tiled=True)  133 us
    unnamed x1, blocking collectives  84.4 us
    all_gather x1, blocking collectives, body(): lax.all_gather(state_part, 'seq')  39.9 us
    all_gather x1, blocking collectives, body(): lax.all_gather(state_rows, 'dp', axis=0, tiled=True)  32.2 us
    all_gather x1, blocking collectives, body(): lax.all_gather(beam_nodes, 'dp', axis=0, tiled=True)  32.1 us
    gather x3, local copies, waits for them, and re-layouts, body(): jnp.take_along_axis(local_scores, jnp.clip(local_rows, 0, nodes_here - 1)...  24.9 us
    gather x2, local copies, waits for them, and re-layouts, body(): stored = jnp.take(subtree_map, all_ids // SUBT) * SUBT + all_ids % SUBT  18.7 us
    another operation x4, local copies, waits for them, and re-layouts  13.8 us
  transfers between devices with their start and end apart: 1, of which 1 were waited for; matrix products, arithmetic and copies ran while one was open for 5% of the time, Pallas kernels for 0%

profile of v1, /device:TPU:0, one launch (start us, length us, event | category | flops | bytes accessed | tf_op | source)
XLA Modules:
  0.0 425.9 jit_solution(1375238597212528578)
XLA Ops:
  7.2 1.2 convert_reduce_fusion
  8.4 1.2 fusion.16
  9.7 5.0 %multiply_convert_fusion = bf16[128,4096]{1,0:T(8,128)(2,1)S(1)} fusion(bf16[1024,4096]{1,0:T(8,128)(2,1)} %param.15, bf16[1,128,1024]{2,1,0:T(8,128)(2,1)} %param.13, f32[1024]{0:T(1024)} %param.14, f32[128]{0:T(128)S(1)} %add_rsqrt_fusion.1, f32[128]{0:T(128)S(1)} %broadcast_multiply_fusion.1), kind=kOutput, calls=%fused_computation.18 | convolution fusion | flops 1077018624 | bytes 9704448 | tf_op jit(solution)/shard_map/dot_general | solution.py:65
  14.6 1.1 copy-done.2
  15.7 0.9 slice.25
  16.6 0.2 reduce-window.4
  16.9 0.1 convert_reduce_fusion.1
  17.1 0.1 select_reduce_fusion.1
  17.3 1.0 fusion.12
  19.0 32.1 %all-gather.1 = s32[16,3,64]{2,1,0:T(4,128)S(1)} all-gather(s32[1,3,64]{2,1,0:T(4,128)S(1)} %bitcast.98), channel_id=1, replica_groups=mesh['dp'=16,'seq'=16] {'dp'}, dimensions={0}, use_global_device_ids=true | all-gather | bytes 13056 | tf_op jit(solution)/shard_map/all_gather | solution.py:104
  51.2 18.7 %gather_fusion = s32[3072]{0:T(1024)S(1)} fusion(s32[64]{0:T(128)S(1)} %copy-done.1, s32[3072]{0:T(1024)S(1)} %broadcast_clamp_fusion), kind=kCustom, calls=%fused_computation | custom fusion | bytes 36864 | tf_op jit(solution)/shard_map/jit(_take)/gather | solution.py:107
  70.1 0.6 dynamic-slice
  71.3 132.7 %all-gather.6.cloned.1.call-done = bf16[2048,2048]{1,0:T(8,128)(2,1)} async-done(((bf16[128,2048]{1,0:T(8,128)(2,1)}), bf16[2048,2048]{1,0:T(8,128)(2,1)}) %all-gather.6.cloned.1.call-update) | async-done | bytes 8388624 | tf_op jit(solution)/shard_map/all_gather | solution.py:74
  204.1 29.9 %conditional.1 = (f32[128,8,128]{2,0,1:T(8,128)S(1)}) conditional(s32[]{:T(128)} %convert_element_type.51, () %tuple.14, (s32[128]{0:T(128)S(1)}, s32[128]{0:T(128)S(1)}, s32[128]{0:T(128)S(1)}, s32[128]{0:T(128)S(1)}, s32[128]{0:T(128)S(1)}, /*index=5*/s32[2048]{0:T(1024)S(1)}, s32[2048]{0:T(1024)S(1)}, s32[2048]{0:T(1024)S(1)}, ...), branch_computations={%region_10.11_spmd, %region_11.12_spmd} | conditional | flops 1094726528 | bytes 52245316 | solution.py:88
  204.1 12.4 %copy.31 = bf16[2048,2048]{0,1:T(8,128)(2,1)} copy(bf16[2048,2048]{1,0:T(8,128)(2,1)} %get-tuple-element.114) | data formatting | bytes 16777216 | tf_op jit(solution)/shard_map
  216.5 6.1 %fusion.52 = (bf16[2048,1024]{0,1:T(8,128)(2,1)}, bf16[2048,1024]{0,1:T(8,128)(2,1)}) fusion(bf16[2048,2048]{0,1:T(8,128)(2,1)} %copy.31), kind=kLoop, calls=%fused_computation.108 | loop fusion | bytes 16777216 | tf_op jit(solution)/shard_map/cond/branch_1_fun/slice | solution.py:82
  222.6 1.4 copy.30
  224.0 1.0 slice.22
  225.0 1.6 fusion.3
  226.6 0.4 fusion.4
  227.0 7.0 %fusion.1 = f32[128,8,128]{2,0,1:T(8,128)S(1)} fusion(bf16[2048,8,128]{0,2,1:T(8,128)(2,1)} %bitcast.94, bf16[128,8,128]{0,2,1:T(8,128)(2,1)S(1)} %bitcast.96, bf16[2048,8,128]{0,2,1:T(8,128)(2,1)} %bitcast.93, f32[128,2048]{1,0:T(8,128)} %fusion.3, f32[8]{0:T(128)S(1)} %get-tuple-element.73, pred[128,2048]{1,0:T(8,128)(4,1)S(1)} %fusion.4), kind=kOutput, calls=%fused_computation.6 | convolution fusion | flops 1092616192 | bytes 10485792 | tf_op jit(solution)/shard_map/cond/branch_1_fun/hqk,khd->qhd/dot_general | solution.py:41
  234.0 0.1 reduce_sum.107
  234.1 0.2 multiply_reduce_fusion
  234.4 1.5 fusion.10
  235.9 0.7 copy-done.6
  236.6 0.2 convolution_bitcast_fusion
  236.8 39.9 %all-gather.2 = f32[16,3,1024]{2,1,0:T(4,128)S(1)} all-gather(f32[1,3,1024]{2,1,0:T(4,128)S(1)} %convolution_bitcast_fusion), channel_id=2, replica_groups=mesh['dp'=16,'seq'=16] {'seq'}, dimensions={0}, use_global_device_ids=true | all-gather | bytes 208896 | tf_op jit(solution)/shard_map/all_gather | solution.py:101
  276.8 32.2 %all-gather.3 = bf16[16,3,1024]{2,1,0:T(4,128)(2,1)S(1)} all-gather(bf16[1,3,1024]{2,1,0:T(4,128)(2,1)S(1)} %bitcast.97), channel_id=1, replica_groups=mesh['dp'=16,'seq'=16] {'dp'}, dimensions={0}, use_global_device_ids=true | all-gather | bytes 104448 | tf_op jit(solution)/shard_map/all_gather | solution.py:103
  309.0 0.3 fusion.53
  309.3 24.7 %gather_fusion.1 = f32[3072]{0:T(1024)S(1)} fusion(f32[48,256]{1,0:T(8,128)S(1)} %fusion.53, s32[3072]{0:T(1024)S(1)} %reshape.285), kind=kCustom, calls=%fused_computation.1 | custom fusion | bytes 49152 | tf_op jit(solution)/shard_map/jit(take_along_axis)/gather | solution.py:113
  334.1 84.4 %all-reduce = f32[48,64]{1,0:T(8,128)S(1)} all-reduce(f32[48,64]{1,0:T(8,128)S(1)} %select_select_fusion), channel_id=3, replica_groups=mesh['dp'=16,'seq'=16] {'dp'}, use_global_device_ids=true, to_apply=%region_15.16.clone | all-reduce | flops 3072 | bytes 24576
  418.5 0.6 constant_dynamic-slice_fusion
  (56 shorter events, 0.9 us)
Async XLA Ops:
  7.2 227.2 %copy-start = (bf16[1024,1024]{1,0:T(8,128)(2,1)S(1)}, bf16[1024,1024]{1,0:T(8,128)(2,1)}, u32[]{:S(2)}) copy-start(bf16[1024,1024]{1,0:T(8,128)(2,1)} %param.17) | copy-start | bytes 6291460
  7.2 196.9 %all-gather.6.cloned.1.call-start = ((), (), s32[]{:S(2)}) async-start(), calls=%async_computation | async-start | bytes 8912896 | tf_op jit(solution)/shard_map/all_gather | solution.py:74
  9.6 7.0 %copy-start.10 = (s32[1,3]{1,0:T(1,128)S(1)}, s32[1,3]{1,0:T(1,128)}, u32[]{:S(2)}) copy-start(s32[1,3]{1,0:T(1,128)} %param.19) | copy-start | bytes 40
  9.6 7.2 %copy-start.9 = (s32[1,3]{1,0:T(1,128)S(1)}, s32[1,3]{1,0:T(1,128)}, u32[]{:S(2)}) copy-start(s32[1,3]{1,0:T(1,128)} %param.20) | copy-start | bytes 40
  9.6 9.3 %copy-start.8 = (s32[3,64]{1,0:T(4,128)S(1)}, s32[3,64]{1,0:T(4,128)}, u32[]{:S(2)}) copy-start(s32[3,64]{1,0:T(4,128)} %param.23) | copy-start | bytes 2308
  14.6 1.1 copy-start.2
  15.7 35.5 %copy-start.1 = (s32[64]{0:T(128)S(1)}, s32[64]{0:T(128)}, u32[]{:S(2)}) copy-start(s32[64]{0:T(128)} %param.22) | copy-start | bytes 772
  51.2 18.9 %copy-start.12 = (u32[256]{0:T(256)S(1)}, u32[256]{0:T(256)}, u32[]{:S(2)}) copy-start(u32[256]{0:T(256)} %constant.165) | copy-start | bytes 3076
  51.2 152.9 %copy-start.11 = (f32[8]{0:T(128)S(1)}, f32[8]{0:T(128)}, u32[]{:S(2)}) copy-start(f32[8]{0:T(128)} %param.18) | copy-start | bytes 100
  204.1 30.3 %copy-start.4 = (bf16[1,128,1024]{2,1,0:T(8,128)(2,1)S(1)}, bf16[1,128,1024]{2,1,0:T(8,128)(2,1)}, u32[]{:S(2)}) copy-start(bf16[1,128,1024]{2,1,0:T(8,128)(2,1)} %param.13) | copy-start | bytes 786436
  204.1 30.3 %copy-start.7 = (f32[1024]{0:T(1024)S(1)}, f32[1024]{0:T(1024)}, u32[]{:S(2)}) copy-start(f32[1024]{0:T(1024)} %param.16) | copy-start | bytes 12292
  216.5 6.1 %copy-start.3 = (bf16[128,4096]{1,0:T(8,128)(2,1)S(1)}, bf16[128,4096]{1,0:T(8,128)(2,1)}, u32[]{:S(2)}) copy-start(bf16[128,4096]{1,0:T(8,128)(2,1)} %get-tuple-element.113) | copy-start | bytes 3145732 | tf_op jit(solution)/shard_map/cond
  234.0 75.0 %copy-start.5 = (bf16[256,1024]{1,0:T(8,128)(2,1)S(1)}, bf16[256,1024]{1,0:T(8,128)(2,1)}, u32[]{:S(2)}) copy-start(bf16[256,1024]{1,0:T(8,128)(2,1)} %param.21) | copy-start | bytes 1572868
  235.9 0.7 copy-start.6
Sparse Core Ops, SparseCore 0:
  16.7 187.3 all-gather.5
